TPU v7x, 512 devices: a whole 4x4x16 slice. The times are simulated.
512 devices in a mesh: blk: 128 (over z, x, core), grp: 4 (over y).
Axes of the slice: x: 4, y: 4, z: 16, core: 2. Of those that a mesh axis runs over, the one named last changes fastest.
Arguments:
- checkpoint: bfloat16 [131072, 320], P(('blk', 'grp')), may hold values from -4 to 4
- adjoint_rhs: bfloat16 [131072, 320], P(('blk', 'grp')), may hold values from -6 to 6
- new_position: int32 [131072], P(('blk', 'grp')), may hold values from 0 to 131071, as said below
- old_position: int32 [131072], P(('blk', 'grp')), may hold values from 0 to 131071, as said below
- left_matrix: bfloat16 [320, 320], replicated, may hold values from -0.3125 to 0.3125
- right_matrix: bfloat16 [320, 320], replicated, may hold values from -0.3125 to 0.3125
- face_block: int32 [6, 131072], P(None, ('blk', 'grp')), may hold values from -1 to 131071, as said below
- face_weight: float32 [6, 131072], P(None, ('blk', 'grp')), may hold values from 0.3 to 0.9
- donor_block: int32 [2, 131072], P(None, ('blk', 'grp')), may hold values from 0 to 131071, as said below
- donor_weight: float32 [2, 131072], P(None, ('blk', 'grp')), may hold values from 0.2 to 0.7
Outputs:
- adjoint: float32 [131072, 320], P(('blk', 'grp'))
Inputs may be any that keep to these rules, and one draw needn't show every extreme that they name: `new_position`: A permutation of the block indices that keeps each block's index along grp; the blocks of one device go to 64 devices along blk, exactly 4 blocks to each of them. `old_position`: the inverse permutation of new_position. `face_block`: each entry is -1 or a block of the same grp index whose place in that group's order of blocks (blk index times 256 plus the local index) lies within 256 places of the block's own, taken cyclically. `donor_block`: each donor lies on the device of the same blk index and another grp index, among the first 128 blocks of that device in the new order.
All inputs are finite; a program needn't handle non-finite values.
Results may differ from a plain program's by a relative error of at most 0.0014.
Values may be sent and summed in bfloat16 or wider, within the bound.
A program may use at most 64 MiB of HBM per device.

v0:
```python
import jax
import jax.numpy as jnp
from jax import lax
from jax.sharding import PartitionSpec as P


def passed_along(block, axis, distance):
    devices = range(lax.axis_size(axis))
    route = [((i - distance) % len(devices), i) for i in devices]
    return lax.ppermute(block, axis, route)


def coefficients(state):
    values = state.astype(jnp.float32)
    left_gain = 0.5 * jnp.tanh(values)
    right_gain = 0.4 * jnp.tanh(1.5 * values - 0.5)
    dual_diag = 2.0 + values * values
    return (left_gain, right_gain, dual_diag)


def transposed_apply(
    adjoint, left_gain, right_gain, left_matrix, right_matrix, left_trans, right_trans
):
    rounded = adjoint.astype(jnp.bfloat16)
    first_proj = jnp.dot(rounded, left_matrix, preferred_element_type=jnp.float32)
    second_proj = jnp.dot(rounded, right_trans, preferred_element_type=jnp.float32)
    first_mid = (first_proj * left_gain).astype(jnp.bfloat16)
    second_mid = (second_proj * right_gain).astype(jnp.bfloat16)
    return jnp.dot(first_mid, right_matrix, preferred_element_type=jnp.float32) + jnp.dot(
        second_mid, left_trans, preferred_element_type=jnp.float32
    )


def face_sum(block_pool, face_index, face_valid, face_weight):
    row_count = face_index.shape[1]
    total_face = jnp.zeros((row_count, block_pool.shape[1]), jnp.float32)
    for face_id in range(face_index.shape[0]):
        fetched = jnp.take(block_pool, face_index[face_id], axis=0).reshape(row_count, 5, 4, 4, 4)
        cell_axis = 2 + face_id // 2
        from_cell = 3 if face_id % 2 == 0 else 0
        face_slab = lax.slice_in_dim(fetched, from_cell, from_cell + 1, axis=cell_axis)
        scale_face = jnp.where(face_valid[face_id], face_weight[face_id], 0.0)
        face_slab = face_slab * scale_face.reshape(row_count, 1, 1, 1, 1)
        pad_shape = list(face_slab.shape)
        pad_shape[cell_axis] = 3
        padding = jnp.zeros(pad_shape, jnp.float32)
        if face_id % 2 == 0:
            placed = jnp.concatenate([face_slab, padding], axis=cell_axis)
        else:
            placed = jnp.concatenate([padding, face_slab], axis=cell_axis)
        total_face = total_face + placed.reshape(row_count, block_pool.shape[1])
    return total_face


def fringe_sum(block_pool, donor_index, donor_weight):
    total_fringe = jnp.zeros((donor_index.shape[1], block_pool.shape[1]), jnp.float32)
    for donor_id in range(donor_index.shape[0]):
        fetched = jnp.take(block_pool, donor_index[donor_id], axis=0)
        total_fringe = total_fringe + donor_weight[donor_id][:, None] * fetched
    return total_fringe


def body(
    checkpoint,
    adjoint_rhs,
    new_position,
    old_position,
    left_matrix,
    right_matrix,
    face_block,
    face_weight,
    donor_block,
    donor_weight,
):
    blk_count = lax.axis_size("blk")
    grp_count = lax.axis_size("grp")
    per_device = checkpoint.shape[0]
    capacity = max(2, 2 * per_device // blk_count)
    my_blk = lax.axis_index("blk")
    left_trans = left_matrix.T
    right_trans = right_matrix.T
    target = new_position // per_device // grp_count
    positions = jnp.arange(per_device, dtype=jnp.int32)
    send_rank = jnp.sum(
        (target[:, None] == target[None, :]) & (positions[None, :] < positions[:, None]), axis=1
    )
    send_slot = target * capacity + send_rank
    anchor = old_position // per_device // grp_count
    anchor_local = old_position % per_device
    recv_rank = jnp.sum(
        (anchor[:, None] == anchor[None, :]) & (anchor_local[None, :] < anchor_local[:, None]),
        axis=1,
    )
    recv_slot = anchor * capacity + recv_rank
    face_valid = face_block >= 0
    face_blk = face_block // per_device // grp_count
    face_place = (face_blk - my_blk + 1) % blk_count * per_device + face_block % per_device
    face_local = jnp.where(face_valid, face_place, 0)
    donor_grp = donor_block // per_device % grp_count
    donor_within = donor_block % per_device

    def pack_rows(values, slot_ids):
        buffer = (
            jnp.zeros((blk_count * capacity, values.shape[1]), values.dtype)
            .at[slot_ids]
            .set(values)
        )
        return buffer.reshape(blk_count, capacity, values.shape[1])

    def unpack_rows(received, slot_ids):
        return received.reshape(blk_count * capacity, received.shape[2])[slot_ids]

    got_state, got_rhs = (
        lax.all_to_all(
            pack_rows(checkpoint, send_slot), "blk", split_axis=0, concat_axis=0, tiled=True
        ),
        lax.all_to_all(
            pack_rows(adjoint_rhs, send_slot), "blk", split_axis=0, concat_axis=0, tiled=True
        ),
    )
    state_new = unpack_rows(got_state, recv_slot)
    rhs_float = unpack_rows(got_rhs, recv_slot).astype(jnp.float32)
    left_gain, right_gain, dual_diag = coefficients(state_new)
    result = rhs_float / dual_diag
    for sweep_step in range(2):
        applied = transposed_apply(
            result, left_gain, right_gain, left_matrix, right_matrix, left_trans, right_trans
        )
        below_adj = passed_along(result.astype(jnp.bfloat16), "blk", 1).astype(result.dtype)
        above_adj = passed_along(result.astype(jnp.bfloat16), "blk", -1).astype(result.dtype)
        block_pool = jnp.concatenate([below_adj, result, above_adj], axis=0)
        face_term = face_sum(block_pool, face_local, face_valid, face_weight)
        group_pool = lax.all_gather(result, "grp", axis=0, tiled=True)
        donor_local = donor_grp * per_device + donor_within
        fringe_term = fringe_sum(group_pool, donor_local, donor_weight)
        face_term, fringe_term = (face_term, fringe_term)
        result = (rhs_float - applied - face_term - fringe_term) / dual_diag
    return result


def solution(mesh):
    in_specs = (
        P(("blk", "grp"), None),
        P(("blk", "grp"), None),
        P(("blk", "grp")),
        P(("blk", "grp")),
        P(),
        P(),
        P(None, ("blk", "grp")),
        P(None, ("blk", "grp")),
        P(None, ("blk", "grp")),
        P(None, ("blk", "grp")),
    )
    out_specs = P(("blk", "grp"), None)
    return jax.shard_map(body, mesh=mesh, in_specs=in_specs, out_specs=out_specs, check_vma=False)
```

profile of v0, /device:TPU:2, one launch (start us, length us, event | category | flops | bytes accessed | tf_op | source)
XLA Modules:
  0.0 188.3 jit_solution(17737311999590870322)
XLA Ops:
  6.5 0.7 and_select_fusion.6
  7.3 0.2 convert_reduce_fusion.1
  7.5 0.7 compare_select_fusion.11
  8.2 1.1 copy.83
  9.3 1.6 scatter_custom_fusion.1
  10.9 0.9 reshape.182
  11.7 19.6 %all-to-all-start.1 = ((bf16[128,4,320]{2,1,0:T(4,128)(2,1)}), bf16[128,4,320]{2,1,0:T(4,128)(2,1)S(1)}, u32[]{:S(2)}, u32[]{:S(2)}) async-start(bf16[128,4,320]{2,1,0:T(4,128)(2,1)} %reshape.182), calls=%async_computation.1 | async-start | bytes 786432 | tf_op jit(solution)/shard_map/all_to_all | solution.py:114
  31.3 0.2 convert_reduce_fusion
  31.8 1.6 scatter_custom_fusion
  33.4 0.9 reshape.180
  34.7 22.8 %all-to-all-done.1 = bf16[128,4,320]{2,1,0:T(4,128)(2,1)S(1)} async-done(((bf16[128,4,320]{2,1,0:T(4,128)(2,1)}), bf16[128,4,320]{2,1,0:T(4,128)(2,1)S(1)}, u32[]{:S(2)}, u32[]{:S(2)}) %all-to-all-start.1) | async-done | bytes 327712 | tf_op jit(solution)/shard_map/all_to_all | solution.py:114
  57.6 8.0 %all-to-all-start = ((bf16[128,4,320]{2,1,0:T(4,128)(2,1)}), bf16[128,4,320]{2,1,0:T(4,128)(2,1)S(1)}, u32[]{:S(2)}, u32[]{:S(2)}) async-start(bf16[128,4,320]{2,1,0:T(4,128)(2,1)} %reshape.180), calls=%async_computation | async-start | bytes 786432 | tf_op jit(solution)/shard_map/all_to_all | solution.py:117
  65.9 0.2 reshape.183
  66.1 1.2 gather_fusion.1
  67.4 24.5 %all-to-all-done = bf16[128,4,320]{2,1,0:T(4,128)(2,1)S(1)} async-done(((bf16[128,4,320]{2,1,0:T(4,128)(2,1)}), bf16[128,4,320]{2,1,0:T(4,128)(2,1)S(1)}, u32[]{:S(2)}, u32[]{:S(2)}) %all-to-all-start) | async-done | bytes 327712 | tf_op jit(solution)/shard_map/all_to_all | solution.py:117
  91.9 0.2 reshape.181
  92.1 1.2 gather_fusion
  93.4 0.8 convert_divide_fusion
  94.2 2.9 %collective-permute-start = (bf16[256,320]{0,1:T(8,128)(2,1)S(1)}, bf16[256,320]{0,1:T(8,128)(2,1)S(1)}, u32[]{:S(2)}, u32[]{:S(2)}) collective-permute-start(bf16[256,320]{0,1:T(8,128)(2,1)S(1)} %get-tuple-element.8), channel_id=1, source_target_pairs={{508,0},{0,4},{4,8},{8,12},{12,16},{16,20},{20,24},{24,28},{28,32}... | collective-permute-start | bytes 491528 | tf_op jit(solution)/shard_map/ppermute | solution.py:10
  97.1 2.7 %collective-permute-start.1 = (bf16[256,320]{0,1:T(8,128)(2,1)S(1)}, bf16[256,320]{0,1:T(8,128)(2,1)S(1)}, u32[]{:S(2)}, u32[]{:S(2)}) collective-permute-start(bf16[256,320]{0,1:T(8,128)(2,1)S(1)} %get-tuple-element.8), channel_id=1, source_target_pairs={{4,0},{8,4},{12,8},{16,12},{20,16},{24,20},{28,24},{32,28},{36,32}... | collective-permute-start | bytes 491528 | tf_op jit(solution)/shard_map/ppermute | solution.py:10
  99.8 0.2 all-gather.5.cloned.1.call-start
  100.0 1.4 fusion.13
  101.4 1.1 collective-permute-done.1
  102.7 0.4 copy.85
  103.1 1.0 gather_fusion.2
  104.4 1.0 gather_fusion.3
  105.8 1.0 gather_fusion.4
  107.1 0.8 reshape.186
  107.9 1.0 gather_fusion.5
  109.2 0.8 reshape.187
  110.0 1.0 gather_fusion.6
  111.2 0.8 reshape.188
  112.1 1.0 gather_fusion.7
  113.5 1.0 slice_multiply_fusion.8
  114.5 1.1 slice_multiply_fusion.6
  115.7 0.2 pad_add_fusion.1
  116.0 12.3 %all-gather.3.cloned.1.call-done = f32[1024,320]{0,1:T(8,128)} async-done(((f32[256,320]{0,1:T(8,128)}), f32[1024,320]{0,1:T(8,128)}) %all-gather.3.cloned.1.call-update) | async-done | bytes 1310736 | tf_op jit(solution)/shard_map/all_gather | solution.py:133
  128.3 1.8 copy.97
  130.1 1.0 gather_fusion.9
  131.2 1.0 gather_fusion.8
  132.5 2.5 %fusion.66 = (bf16[256,320]{0,1:T(8,128)(2,1)S(1)}, f32[256,320]{0,1:T(8,128)}) fusion(bf16[256,320]{0,1:T(8,128)(2,1)S(1)} %copy.84, f32[256,320]{0,1:T(8,128)S(1)} %copy.100, pred[256]{0:T(512)(128)(4,1)S(1)} %get-tuple-element.35, f32[256]{0:T(256)S(1)} %bitcast.84, f32[256,320]{0,1:T(8,128)S(1)} %copy.98, pred[256]{0:T(512)(128)(4,1)S(1)} %get-tuple-element.36, ...), kind=kOutput, calls=%fused_computation.198 | convolution fusion | flops 107069440 | bytes 2542080 | tf_op jit(solution)/shard_map/dot_general | solution.py:29
  135.0 1.9 %collective-permute-start.2 = (bf16[256,320]{0,1:T(8,128)(2,1)S(1)}, bf16[256,320]{0,1:T(8,128)(2,1)S(1)}, u32[]{:S(2)}, u32[]{:S(2)}) collective-permute-start(bf16[256,320]{0,1:T(8,128)(2,1)S(1)} %get-tuple-element.27), channel_id=1, source_target_pairs={{508,0},{0,4},{4,8},{8,12},{12,16},{16,20},{20,24},{24,28},{28,32}... | collective-permute-start | bytes 491528 | tf_op jit(solution)/shard_map/ppermute | solution.py:10
  136.9 3.9 %collective-permute-start.3 = (bf16[256,320]{0,1:T(8,128)(2,1)S(1)}, bf16[256,320]{0,1:T(8,128)(2,1)S(1)}, u32[]{:S(2)}, u32[]{:S(2)}) collective-permute-start(bf16[256,320]{0,1:T(8,128)(2,1)S(1)} %get-tuple-element.27), channel_id=1, source_target_pairs={{4,0},{8,4},{12,8},{16,12},{20,16},{24,20},{28,24},{32,28},{36,32}... | collective-permute-start | bytes 491528 | tf_op jit(solution)/shard_map/ppermute | solution.py:10
  140.8 1.4 fusion.12
  142.2 1.1 collective-permute-done.3
  143.5 0.4 copy.101
  143.8 1.9 gather_fusion.14
  145.7 1.1 gather_fusion.13
  146.8 1.1 gather_fusion.12
  147.9 1.1 gather_fusion.11
  149.1 1.1 gather_fusion.10
  150.2 1.1 gather_fusion.15
  151.3 1.1 broadcast_select_fusion.1
  153.1 0.3 copy-done.43
  153.7 0.3 copy-done.39
  154.4 0.2 copy-done.37
  155.0 0.2 copy-done.41
  155.6 0.2 copy-done.24
  156.4 18.4 %all-gather.5.cloned.1.call-done = f32[1024,320]{0,1:T(8,128)} async-done(((f32[256,320]{0,1:T(8,128)}), f32[1024,320]{0,1:T(8,128)}) %all-gather.5.cloned.1.call-update) | async-done | bytes 1310736 | tf_op jit(solution)/shard_map/all_gather | solution.py:133
  174.9 1.8 copy.113
  176.7 1.1 gather_fusion.16
  177.8 1.1 gather_fusion.17
  179.3 0.5 copy-done.4
  180.1 1.3 fusion.7
  (199 shorter events, 6.5 us)
Async XLA Ops:
  6.5 93.5 %copy-start = (bf16[320,320]{1,0:T(8,128)(2,1)S(1)}, bf16[320,320]{1,0:T(8,128)(2,1)}, u32[]{:S(2)}) copy-start(bf16[320,320]{1,0:T(8,128)(2,1)} %param.19) | copy-start | bytes 614404
  6.5 24.8 %copy-start.47 = (s32[256]{0:T(256)S(1)}, s32[256]{0:T(256)}, u32[]{:S(2)}) copy-start(s32[256]{0:T(256)} %param.17) | copy-start | bytes 3076
  6.5 25.0 %copy-start.11 = (bf16[256,320]{0,1:T(8,128)(2,1)S(1)}, bf16[256,320]{0,1:T(8,128)(2,1)}, u32[]{:S(2)}) copy-start(bf16[256,320]{0,1:T(8,128)(2,1)} %param.15) | copy-start | bytes 491524
  11.7 22.5 %copy-start.12 = (s32[6,256]{1,0:T(8,128)S(1)}, s32[6,256]{1,0:T(8,128)}, u32[]{:S(2)}) copy-start(s32[6,256]{1,0:T(8,128)} %param.20) | copy-start | bytes 18436
  11.7 22.8 %copy-start.34 = (s32[2,256]{1,0:T(2,128)S(1)}, s32[2,256]{1,0:T(2,128)}, u32[]{:S(2)}) copy-start(s32[2,256]{1,0:T(2,128)} %param.22) | copy-start | bytes 6148
  11.7 45.8 %all-to-all-start.1 = ((bf16[128,4,320]{2,1,0:T(4,128)(2,1)}), bf16[128,4,320]{2,1,0:T(4,128)(2,1)S(1)}, u32[]{:S(2)}, u32[]{:S(2)}) async-start(bf16[128,4,320]{2,1,0:T(4,128)(2,1)} %reshape.182), calls=%async_computation.1 | async-start | bytes 786432 | tf_op jit(solution)/shard_map/all_to_all | solution.py:114
  31.6 34.2 %copy-start.35 = (f32[2,256]{1,0:T(2,128)S(1)}, f32[2,256]{1,0:T(2,128)}, u32[]{:S(2)}) copy-start(f32[2,256]{1,0:T(2,128)} %param.23) | copy-start | bytes 6148
  31.6 34.2 %copy-start.33 = (f32[6,256]{1,0:T(8,128)S(1)}, f32[6,256]{1,0:T(8,128)}, u32[]{:S(2)}) copy-start(f32[6,256]{1,0:T(8,128)} %param.21) | copy-start | bytes 18436
  34.3 68.7 %copy-start.27 = (s32[1024]{0:T(1024)}, s32[1024]{0:T(1024)S(1)}, u32[]{:S(2)}) copy-start(s32[1024]{0:T(1024)S(1)} %pad_clamp_fusion.7) | copy-start | bytes 12292
  34.4 70.1 %copy-start.28 = (s32[1024]{0:T(1024)}, s32[1024]{0:T(1024)S(1)}, u32[]{:S(2)}) copy-start(s32[1024]{0:T(1024)S(1)} %pad_clamp_fusion.6) | copy-start | bytes 12292
  34.4 71.4 %copy-start.29 = (s32[1024]{0:T(1024)}, s32[1024]{0:T(1024)S(1)}, u32[]{:S(2)}) copy-start(s32[1024]{0:T(1024)S(1)} %pad_clamp_fusion.5) | copy-start | bytes 12292
  34.4 73.4 %copy-start.31 = (s32[1024]{0:T(1024)}, s32[1024]{0:T(1024)S(1)}, u32[]{:S(2)}) copy-start(s32[1024]{0:T(1024)S(1)} %pad_clamp_fusion.4) | copy-start | bytes 12292
  34.5 75.5 %copy-start.32 = (s32[1024]{0:T(1024)}, s32[1024]{0:T(1024)S(1)}, u32[]{:S(2)}) copy-start(s32[1024]{0:T(1024)S(1)} %pad_clamp_fusion.3) | copy-start | bytes 12292
  34.5 77.5 %copy-start.30 = (s32[1024]{0:T(1024)}, s32[1024]{0:T(1024)S(1)}, u32[]{:S(2)}) copy-start(s32[1024]{0:T(1024)S(1)} %pad_clamp_fusion.2) | copy-start | bytes 12292
  34.6 95.5 %copy-start.25 = (s32[1024]{0:T(1024)}, s32[1024]{0:T(1024)S(1)}, u32[]{:S(2)}) copy-start(s32[1024]{0:T(1024)S(1)} %pad_clamp_fusion) | copy-start | bytes 12292
  34.6 96.6 %copy-start.26 = (s32[1024]{0:T(1024)}, s32[1024]{0:T(1024)S(1)}, u32[]{:S(2)}) copy-start(s32[1024]{0:T(1024)S(1)} %pad_clamp_fusion.1) | copy-start | bytes 12292
  34.7 69.4 %copy-start.36 = (pred[256]{0:T(512)(128)(4,1)}, pred[256]{0:T(512)(128)(4,1)S(1)}, u32[]{:S(2)}) copy-start(pred[256]{0:T(512)(128)(4,1)S(1)} %compare_and_fusion.7) | copy-start | bytes 772
  34.7 70.7 %copy-start.38 = (pred[256]{0:T(512)(128)(4,1)}, pred[256]{0:T(512)(128)(4,1)S(1)}, u32[]{:S(2)}) copy-start(pred[256]{0:T(512)(128)(4,1)S(1)} %compare_and_fusion.6) | copy-start | bytes 772
  34.7 72.1 %copy-start.42 = (pred[256]{0:T(512)(128)(4,1)}, pred[256]{0:T(512)(128)(4,1)S(1)}, u32[]{:S(2)}) copy-start(pred[256]{0:T(512)(128)(4,1)S(1)} %compare_and_fusion.5) | copy-start | bytes 772
  34.7 74.1 %copy-start.44 = (pred[256]{0:T(512)(128)(4,1)}, pred[256]{0:T(512)(128)(4,1)S(1)}, u32[]{:S(2)}) copy-start(pred[256]{0:T(512)(128)(4,1)S(1)} %compare_and_fusion.4) | copy-start | bytes 772
  57.6 34.3 %all-to-all-start = ((bf16[128,4,320]{2,1,0:T(4,128)(2,1)}), bf16[128,4,320]{2,1,0:T(4,128)(2,1)S(1)}, u32[]{:S(2)}, u32[]{:S(2)}) async-start(bf16[128,4,320]{2,1,0:T(4,128)(2,1)} %reshape.180), calls=%async_computation | async-start | bytes 786432 | tf_op jit(solution)/shard_map/all_to_all | solution.py:117
  65.6 62.7 %all-gather.3.cloned.1.call-start = ((), (), s32[]{:S(2)}) async-start(), calls=%async_computation.2 | async-start | bytes 1638400 | tf_op jit(solution)/shard_map/all_gather | solution.py:133
  65.7 45.3 %copy-start.46 = (pred[256]{0:T(512)(128)(4,1)}, pred[256]{0:T(512)(128)(4,1)S(1)}, u32[]{:S(2)}) copy-start(pred[256]{0:T(512)(128)(4,1)S(1)} %compare_and_fusion.3) | copy-start | bytes 772
  65.7 47.4 %copy-start.40 = (pred[256]{0:T(512)(128)(4,1)}, pred[256]{0:T(512)(128)(4,1)S(1)}, u32[]{:S(2)}) copy-start(pred[256]{0:T(512)(128)(4,1)S(1)} %compare_and_fusion.2) | copy-start | bytes 772
  65.7 66.7 %copy-start.52 = (pred[256]{0:T(512)(128)(4,1)}, pred[256]{0:T(512)(128)(4,1)S(1)}, u32[]{:S(2)}) copy-start(pred[256]{0:T(512)(128)(4,1)S(1)} %get-tuple-element.35) | copy-start | bytes 772
  65.7 66.7 %copy-start.54 = (pred[256]{0:T(512)(128)(4,1)}, pred[256]{0:T(512)(128)(4,1)S(1)}, u32[]{:S(2)}) copy-start(pred[256]{0:T(512)(128)(4,1)S(1)} %get-tuple-element.36) | copy-start | bytes 772
  65.8 66.6 %copy-start.48 = (f32[1,256]{1,0:T(1,128)}, f32[1,256]{1,0:T(1,128)S(1)}, u32[]{:S(2)}) copy-start(f32[1,256]{1,0:T(1,128)S(1)} %get-tuple-element.21) | copy-start | bytes 3076
  65.8 66.6 %copy-start.50 = (f32[1,256]{1,0:T(1,128)}, f32[1,256]{1,0:T(1,128)S(1)}, u32[]{:S(2)}) copy-start(f32[1,256]{1,0:T(1,128)S(1)} %get-tuple-element.22) | copy-start | bytes 3076
  65.8 47.6 %copy-start.17 = (f32[1,256]{1,0:T(1,128)}, f32[1,256]{1,0:T(1,128)S(1)}, u32[]{:S(2)}) copy-start(f32[1,256]{1,0:T(1,128)S(1)} %get-tuple-element.9) | copy-start | bytes 3076
  65.8 47.6 %copy-start.19 = (f32[1,256]{1,0:T(1,128)}, f32[1,256]{1,0:T(1,128)S(1)}, u32[]{:S(2)}) copy-start(f32[1,256]{1,0:T(1,128)S(1)} %get-tuple-element.13) | copy-start | bytes 3076
  65.9 47.6 %copy-start.21 = (f32[1,256]{1,0:T(1,128)}, f32[1,256]{1,0:T(1,128)S(1)}, u32[]{:S(2)}) copy-start(f32[1,256]{1,0:T(1,128)S(1)} %get-tuple-element.12) | copy-start | bytes 3076
  65.9 47.6 %copy-start.23 = (f32[1,256]{1,0:T(1,128)}, f32[1,256]{1,0:T(1,128)S(1)}, u32[]{:S(2)}) copy-start(f32[1,256]{1,0:T(1,128)S(1)} %get-tuple-element.11) | copy-start | bytes 3076
  65.9 48.6 %copy-start.13 = (f32[1,256]{1,0:T(1,128)}, f32[1,256]{1,0:T(1,128)S(1)}, u32[]{:S(2)}) copy-start(f32[1,256]{1,0:T(1,128)S(1)} %get-tuple-element.14) | copy-start | bytes 3076
  65.9 48.6 %copy-start.15 = (f32[1,256]{1,0:T(1,128)}, f32[1,256]{1,0:T(1,128)S(1)}, u32[]{:S(2)}) copy-start(f32[1,256]{1,0:T(1,128)S(1)} %get-tuple-element.10) | copy-start | bytes 3076
  93.2 6.8 %copy-start.6 = (bf16[320,320]{1,0:T(8,128)(2,1)S(1)}, bf16[320,320]{1,0:T(8,128)(2,1)}, u32[]{:S(2)}) copy-start(bf16[320,320]{1,0:T(8,128)(2,1)} %param.18) | copy-start | bytes 614404
  93.4 39.0 %copy-start.3 = (bf16[256,320]{0,1:T(8,128)(2,1)}, bf16[256,320]{0,1:T(8,128)(2,1)S(1)}, u32[]{:S(2)}) copy-start(bf16[256,320]{0,1:T(8,128)(2,1)S(1)} %copy.82) | copy-start | bytes 491524
  94.2 7.2 %collective-permute-start = (bf16[256,320]{0,1:T(8,128)(2,1)S(1)}, bf16[256,320]{0,1:T(8,128)(2,1)S(1)}, u32[]{:S(2)}, u32[]{:S(2)}) collective-permute-start(bf16[256,320]{0,1:T(8,128)(2,1)S(1)} %get-tuple-element.8), channel_id=1, source_target_pairs={{508,0},{0,4},{4,8},{8,12},{12,16},{16,20},{20,24},{24,28},{28,32}... | collective-permute-start | bytes 491528 | tf_op jit(solution)/shard_map/ppermute | solution.py:10
  97.1 5.5 %collective-permute-start.1 = (bf16[256,320]{0,1:T(8,128)(2,1)S(1)}, bf16[256,320]{0,1:T(8,128)(2,1)S(1)}, u32[]{:S(2)}, u32[]{:S(2)}) collective-permute-start(bf16[256,320]{0,1:T(8,128)(2,1)S(1)} %get-tuple-element.8), channel_id=1, source_target_pairs={{4,0},{8,4},{12,8},{16,12},{20,16},{24,20},{28,24},{32,28},{36,32}... | collective-permute-start | bytes 491528 | tf_op jit(solution)/shard_map/ppermute | solution.py:10
  99.8 2.8 %copy-start.1 = (f32[256,320]{0,1:T(8,128)S(1)}, f32[256,320]{0,1:T(8,128)}, u32[]{:S(2)}) copy-start(f32[256,320]{0,1:T(8,128)} %get-tuple-element.6) | copy-start | bytes 983044
  99.8 75.1 %all-gather.5.cloned.1.call-start = ((), (), s32[]{:S(2)}) async-start(), calls=%async_computation.3 | async-start | bytes 1638400 | tf_op jit(solution)/shard_map/all_gather | solution.py:133
  132.4 8.3 %copy-start.7 = (bf16[320,320]{1,0:T(8,128)(2,1)S(1)}, bf16[320,320]{1,0:T(8,128)(2,1)}, u32[]{:S(2)}) copy-start(bf16[320,320]{1,0:T(8,128)(2,1)} %param.18) | copy-start | bytes 614404
  135.0 8.4 %copy-start.9 = (bf16[256,320]{0,1:T(8,128)(2,1)}, bf16[256,320]{0,1:T(8,128)(2,1)S(1)}, u32[]{:S(2)}) copy-start(bf16[256,320]{0,1:T(8,128)(2,1)S(1)} %get-tuple-element.27) | copy-start | bytes 491524
  135.0 7.2 %collective-permute-start.2 = (bf16[256,320]{0,1:T(8,128)(2,1)S(1)}, bf16[256,320]{0,1:T(8,128)(2,1)S(1)}, u32[]{:S(2)}, u32[]{:S(2)}) collective-permute-start(bf16[256,320]{0,1:T(8,128)(2,1)S(1)} %get-tuple-element.27), channel_id=1, source_target_pairs={{508,0},{0,4},{4,8},{8,12},{12,16},{16,20},{20,24},{24,28},{28,32}... | collective-permute-start | bytes 491528 | tf_op jit(solution)/shard_map/ppermute | solution.py:10
  136.9 6.5 %collective-permute-start.3 = (bf16[256,320]{0,1:T(8,128)(2,1)S(1)}, bf16[256,320]{0,1:T(8,128)(2,1)S(1)}, u32[]{:S(2)}, u32[]{:S(2)}) collective-permute-start(bf16[256,320]{0,1:T(8,128)(2,1)S(1)} %get-tuple-element.27), channel_id=1, source_target_pairs={{4,0},{8,4},{12,8},{16,12},{20,16},{24,20},{28,24},{32,28},{36,32}... | collective-permute-start | bytes 491528 | tf_op jit(solution)/shard_map/ppermute | solution.py:10
  140.7 2.6 %copy-start.2 = (f32[256,320]{0,1:T(8,128)S(1)}, f32[256,320]{0,1:T(8,128)}, u32[]{:S(2)}) copy-start(f32[256,320]{0,1:T(8,128)} %get-tuple-element.28) | copy-start | bytes 983044
  151.3 1.4 copy-start.45
  152.7 0.6 copy-start.43
  153.3 0.7 copy-start.39
  154.0 0.6 copy-start.37
  154.6 0.6 copy-start.41
  155.2 0.6 copy-start.24
  155.2 0.7 copy-start.22
  155.2 0.7 copy-start.20
  155.2 0.7 copy-start.18
  155.3 0.6 copy-start.16
  155.3 0.7 copy-start.14
  178.9 0.9 copy-start.4
  178.9 1.1 copy-start.5
  178.9 1.1 copy-start.8
  178.9 1.2 copy-start.10
  178.9 1.2 copy-start.49
  179.0 1.2 copy-start.51
  179.0 1.2 copy-start.53
  179.0 1.2 copy-start.55
Sparse Core Ops, SparseCore 0:
  99.9 28.3 all-gather.2
  140.9 33.9 all-gather.4
where the time goes:
time: 189 us; the launch traced here: 188 us
  waiting for transfers between devices  80.4 us (43%)
  local copies, waits for them, and re-layouts  39.3 us (21%)
  starting transfers between devices  39.2 us (21%)
  between operations  14.9 us (8%)
  other arithmetic  8.04 us (4%)
  matrix products  6.58 us (3%)
    all_gather x2, waiting for transfers between devices, body(): group_pool = lax.all_gather(result, 'grp', axis=0, tiled=True)  30.8 us
    all_to_all x1, waiting for transfers between devices, body(): lax.all_to_all(pack_rows(adjoint_rhs, send_slot), 'blk', split_axis=0, co...  24.5 us
    all_to_all x1, waiting for transfers between devices, body(): lax.all_to_all(pack_rows(checkpoint, send_slot), 'blk', split_axis=0, con...  22.8 us
    all_to_all x1, starting transfers between devices, body(): lax.all_to_all(pack_rows(checkpoint, send_slot), 'blk', split_axis=0, con...  19.6 us
    gather x12, local copies, waits for them, and re-layouts, face_sum(): jnp.take(block_pool, face_index[face_id], axis=0)  13.4 us
    ppermute x4, starting transfers between devices, passed_along(): return lax.ppermute(block, axis, route)  11.3 us
    all_to_all x1, starting transfers between devices, body(): lax.all_to_all(pack_rows(adjoint_rhs, send_slot), 'blk', split_axis=0, co...  8.05 us
    gather x8, local copies, waits for them, and re-layouts, fringe_sum(): fetched = jnp.take(block_pool, donor_index[donor_id], axis=0)  4.8 us
  transfers between devices with their start and end apart: 8, of which 6 were waited for; matrix products, arithmetic and copies ran while one was open for 17% of the time, Pallas kernels for 0%

commit v1 on v0

--- a/solution.py
+++ b/solution.py
@@ -130,7 +130,8 @@
         above_adj = passed_along(result.astype(jnp.bfloat16), "blk", -1).astype(result.dtype)
         block_pool = jnp.concatenate([below_adj, result, above_adj], axis=0)
         face_term = face_sum(block_pool, face_local, face_valid, face_weight)
-        group_pool = lax.all_gather(result, "grp", axis=0, tiled=True)
+        repeated = jnp.stack([result] * lax.axis_size("grp"))
+        group_pool = jnp.concatenate(lax.all_to_all(repeated, "grp", 0, 0), axis=0)
         donor_local = donor_grp * per_device + donor_within
         fringe_term = fringe_sum(group_pool, donor_local, donor_weight)
         face_term, fringe_term = (face_term, fringe_term)

time: 189 us -> 170 us (0.90)
  the two profiles are of different devices: /device:TPU:2 before, /device:TPU:8 now
where the time goes in v1:
time: 170 us; the launch traced here: 169 us
  starting transfers between devices  56.2 us (33%)
  local copies, waits for them, and re-layouts  48.5 us (29%)
  waiting for transfers between devices  38.6 us (23%)
  other arithmetic  19.1 us (11%)
  matrix products  5.66 us (3%)
    all_to_all x1, waiting for transfers between devices, body(): lax.all_to_all(pack_rows(adjoint_rhs, send_slot), 'blk', split_axis=0, co...  21.9 us
    all_to_all x1, starting transfers between devices, body(): lax.all_to_all(pack_rows(checkpoint, send_slot), 'blk', split_axis=0, con...  19.9 us
    ppermute x4, starting transfers between devices, passed_along(): return lax.ppermute(block, axis, route)  17.8 us
    gather x12, local copies, waits for them, and re-layouts, face_sum(): jnp.take(block_pool, face_index[face_id], axis=0)  16.9 us
    all_to_all x1, waiting for transfers between devices, body(): lax.all_to_all(pack_rows(checkpoint, send_slot), 'blk', split_axis=0, con...  16.7 us
    all_to_all x2, starting transfers between devices, body(): group_pool = jnp.concatenate(lax.all_to_all(repeated, 'grp', 0, 0), axis=0)  9.84 us
    all_to_all x1, starting transfers between devices, body(): lax.all_to_all(pack_rows(adjoint_rhs, send_slot), 'blk', split_axis=0, co...  8.71 us
    reshape x12, local copies, waits for them, and re-layouts, face_sum(): jnp.take(block_pool, face_index[face_id], axis=0)  5.47 us
  transfers between devices with their start and end apart: 8, of which 2 were waited for; matrix products, arithmetic and copies ran while one was open for 33% of the time, Pallas kernels for 0%

profile of v1, /device:TPU:8, one launch (start us, length us, event | category | flops | bytes accessed | tf_op | source)
XLA Modules:
  0.0 169.2 jit_solution(15859565760449419995)
XLA Ops:
  0.0 0.7 and_select_fusion.6
  0.9 0.7 compare_select_fusion.11
  1.6 1.1 copy.113
  2.7 1.6 scatter_custom_fusion.1
  4.3 0.9 reshape.193
  5.2 19.9 %all-to-all-start.1 = ((bf16[128,4,320]{2,1,0:T(4,128)(2,1)}), bf16[128,4,320]{2,1,0:T(4,128)(2,1)S(1)}, u32[]{:S(2)}, u32[]{:S(2)}) async-start(bf16[128,4,320]{2,1,0:T(4,128)(2,1)} %reshape.193), calls=%async_computation.1 | async-start | bytes 786432 | tf_op jit(solution)/shard_map/all_to_all | solution.py:114
  25.6 1.6 scatter_custom_fusion
  27.2 0.9 reshape.191
  28.2 0.6 pad_clamp_fusion.6
  28.8 0.6 pad_clamp_fusion.5
  29.4 0.6 pad_clamp_fusion.4
  30.0 0.6 pad_clamp_fusion.3
  30.6 0.6 pad_clamp_fusion.2
  33.5 0.6 compare_and_fusion.4
  34.1 16.7 %all-to-all-done.1 = bf16[128,4,320]{2,1,0:T(4,128)(2,1)S(1)} async-done(((bf16[128,4,320]{2,1,0:T(4,128)(2,1)}), bf16[128,4,320]{2,1,0:T(4,128)(2,1)S(1)}, u32[]{:S(2)}, u32[]{:S(2)}) %all-to-all-start.1) | async-done | bytes 327712 | tf_op jit(solution)/shard_map/all_to_all | solution.py:114
  50.8 8.7 %all-to-all-start = ((bf16[128,4,320]{2,1,0:T(4,128)(2,1)}), bf16[128,4,320]{2,1,0:T(4,128)(2,1)S(1)}, u32[]{:S(2)}, u32[]{:S(2)}) async-start(bf16[128,4,320]{2,1,0:T(4,128)(2,1)} %reshape.191), calls=%async_computation | async-start | bytes 786432 | tf_op jit(solution)/shard_map/all_to_all | solution.py:117
  61.9 1.2 gather_fusion.1
  63.2 21.9 %all-to-all-done = bf16[128,4,320]{2,1,0:T(4,128)(2,1)S(1)} async-done(((bf16[128,4,320]{2,1,0:T(4,128)(2,1)}), bf16[128,4,320]{2,1,0:T(4,128)(2,1)S(1)}, u32[]{:S(2)}, u32[]{:S(2)}) %all-to-all-start) | async-done | bytes 327712 | tf_op jit(solution)/shard_map/all_to_all | solution.py:117
  85.3 1.2 gather_fusion
  86.7 1.9 %collective-permute-start = (bf16[256,320]{0,1:T(8,128)(2,1)S(1)}, bf16[256,320]{0,1:T(8,128)(2,1)S(1)}, u32[]{:S(2)}, u32[]{:S(2)}) collective-permute-start(bf16[256,320]{0,1:T(8,128)(2,1)S(1)} %get-tuple-element.8), channel_id=1, source_target_pairs={{508,0},{0,4},{4,8},{8,12},{12,16},{16,20},{20,24},{24,28},{28,32}... | collective-permute-start | bytes 491528 | tf_op jit(solution)/shard_map/ppermute | solution.py:10
  88.6 7.0 %collective-permute-start.1 = (bf16[256,320]{0,1:T(8,128)(2,1)S(1)}, bf16[256,320]{0,1:T(8,128)(2,1)S(1)}, u32[]{:S(2)}, u32[]{:S(2)}) collective-permute-start(bf16[256,320]{0,1:T(8,128)(2,1)S(1)} %get-tuple-element.8), channel_id=1, source_target_pairs={{4,0},{8,4},{12,8},{16,12},{20,16},{24,20},{28,24},{32,28},{36,32}... | collective-permute-start | bytes 491528 | tf_op jit(solution)/shard_map/ppermute | solution.py:10
  95.6 1.2 stack.4
  96.8 5.0 %all-to-all-start.2 = ((f32[4,256,320]{1,2,0:T(8,128)}), f32[4,256,320]{1,2,0:T(8,128)S(1)}, u32[]{:S(2)}, u32[]{:S(2)}) async-start(f32[4,256,320]{1,2,0:T(8,128)} %stack.4), calls=%async_computation.2 | async-start | bytes 2621440 | tf_op jit(solution)/shard_map/all_to_all | solution.py:134
  101.8 1.4 fusion.13
  103.3 1.0 pad_maximum_fusion
  104.3 1.6 copy.115
  105.9 1.0 gather_fusion.2
  107.1 0.8 reshape.195
  107.9 1.3 gather_fusion.3
  109.5 0.8 reshape.196
  110.3 1.3 gather_fusion.4
  111.8 0.8 reshape.197
  112.7 1.3 gather_fusion.5
  114.2 0.8 reshape.198
  115.0 1.3 gather_fusion.6
  116.5 0.8 reshape.199
  117.3 1.3 gather_fusion.7
  119.0 1.0 slice_multiply_fusion.10
  120.0 1.0 slice_multiply_fusion.8
  120.9 1.1 slice_multiply_fusion.6
  122.3 0.8 reshape.211
  123.6 1.0 gather_fusion.8
  124.8 1.3 gather_fusion.9
  126.3 1.6 fusion.66
  127.9 1.9 %collective-permute-start.2 = (bf16[256,320]{0,1:T(8,128)(2,1)S(1)}, bf16[256,320]{0,1:T(8,128)(2,1)S(1)}, u32[]{:S(2)}, u32[]{:S(2)}) collective-permute-start(bf16[256,320]{0,1:T(8,128)(2,1)S(1)} %get-tuple-element.27), channel_id=1, source_target_pairs={{508,0},{0,4},{4,8},{8,12},{12,16},{16,20},{20,24},{24,28},{28,32}... | collective-permute-start | bytes 491528 | tf_op jit(solution)/shard_map/ppermute | solution.py:10
  129.9 7.0 %collective-permute-start.3 = (bf16[256,320]{0,1:T(8,128)(2,1)S(1)}, bf16[256,320]{0,1:T(8,128)(2,1)S(1)}, u32[]{:S(2)}, u32[]{:S(2)}) collective-permute-start(bf16[256,320]{0,1:T(8,128)(2,1)S(1)} %get-tuple-element.27), channel_id=1, source_target_pairs={{4,0},{8,4},{12,8},{16,12},{20,16},{24,20},{28,24},{32,28},{36,32}... | collective-permute-start | bytes 491528 | tf_op jit(solution)/shard_map/ppermute | solution.py:10
  136.8 1.2 stack.5
  138.0 4.8 %all-to-all-start.3 = ((f32[4,256,320]{1,2,0:T(8,128)}), f32[4,256,320]{1,2,0:T(8,128)S(1)}, u32[]{:S(2)}, u32[]{:S(2)}) async-start(f32[4,256,320]{1,2,0:T(8,128)} %stack.5), calls=%async_computation.3 | async-start | bytes 2621440 | tf_op jit(solution)/shard_map/all_to_all | solution.py:134
  142.8 1.3 fusion.12
  144.2 1.0 pad_maximum_fusion.1
  145.3 1.6 copy.130
  146.8 1.9 %gather_fusion.14 = f32[256,320]{1,0:T(8,128)} fusion(f32[768,320]{1,0:T(8,128)S(1)} %copy.130, s32[1024]{0:T(1024)} %pad_clamp_fusion.3), kind=kCustom, calls=%fused_computation.11.clone | custom fusion | bytes 656384 | tf_op jit(solution)/shard_map/jit(_take)/gather | solution.py:38
  148.7 1.9 %gather_fusion.13 = f32[256,320]{1,0:T(8,128)} fusion(f32[768,320]{1,0:T(8,128)S(1)} %copy.130, s32[1024]{0:T(1024)} %pad_clamp_fusion.4), kind=kCustom, calls=%fused_computation.10.clone | custom fusion | bytes 656384 | tf_op jit(solution)/shard_map/jit(_take)/gather | solution.py:38
  150.6 1.9 %gather_fusion.12 = f32[256,320]{1,0:T(8,128)} fusion(f32[768,320]{1,0:T(8,128)S(1)} %copy.130, s32[1024]{0:T(1024)} %pad_clamp_fusion.5), kind=kCustom, calls=%fused_computation.9.clone | custom fusion | bytes 656384 | tf_op jit(solution)/shard_map/jit(_take)/gather | solution.py:38
  152.4 1.9 %gather_fusion.11 = f32[256,320]{1,0:T(8,128)} fusion(f32[768,320]{1,0:T(8,128)S(1)} %copy.130, s32[1024]{0:T(1024)} %pad_clamp_fusion.6), kind=kCustom, calls=%fused_computation.8.clone | custom fusion | bytes 656384 | tf_op jit(solution)/shard_map/jit(_take)/gather | solution.py:38
  154.3 1.1 gather_fusion.10
  155.4 1.1 gather_fusion.15
  156.6 1.1 broadcast_select_fusion.1
  157.9 0.8 reshape.207
  159.4 0.6 slice_multiply_fusion.2
  162.4 1.1 slice_multiply_fusion.1
  164.4 1.1 gather_fusion.16
  165.5 1.1 gather_fusion.17
  167.9 1.3 fusion.7
  (187 shorter events, 13.6 us)
Async XLA Ops:
  0.0 101.8 %copy-start = (bf16[320,320]{1,0:T(8,128)(2,1)S(1)}, bf16[320,320]{1,0:T(8,128)(2,1)}, u32[]{:S(2)}) copy-start(bf16[320,320]{1,0:T(8,128)(2,1)} %param.19) | copy-start | bytes 614404
  0.0 25.1 %copy-start.41 = (s32[256]{0:T(256)S(1)}, s32[256]{0:T(256)}, u32[]{:S(2)}) copy-start(s32[256]{0:T(256)} %param.17) | copy-start | bytes 3076
  0.0 25.4 %copy-start.18 = (bf16[256,320]{0,1:T(8,128)(2,1)S(1)}, bf16[256,320]{0,1:T(8,128)(2,1)}, u32[]{:S(2)}) copy-start(bf16[256,320]{0,1:T(8,128)(2,1)} %param.15) | copy-start | bytes 491524
  5.2 22.9 %copy-start.19 = (s32[6,256]{1,0:T(8,128)S(1)}, s32[6,256]{1,0:T(8,128)}, u32[]{:S(2)}) copy-start(s32[6,256]{1,0:T(8,128)} %param.20) | copy-start | bytes 18436
  5.2 26.0 %copy-start.27 = (s32[2,256]{1,0:T(2,128)S(1)}, s32[2,256]{1,0:T(2,128)}, u32[]{:S(2)}) copy-start(s32[2,256]{1,0:T(2,128)} %param.22) | copy-start | bytes 6148
  5.2 45.5 %all-to-all-start.1 = ((bf16[128,4,320]{2,1,0:T(4,128)(2,1)}), bf16[128,4,320]{2,1,0:T(4,128)(2,1)S(1)}, u32[]{:S(2)}, u32[]{:S(2)}) async-start(bf16[128,4,320]{2,1,0:T(4,128)(2,1)} %reshape.193), calls=%async_computation.1 | async-start | bytes 786432 | tf_op jit(solution)/shard_map/all_to_all | solution.py:114
  25.4 35.6 %copy-start.28 = (f32[2,256]{1,0:T(2,128)S(1)}, f32[2,256]{1,0:T(2,128)}, u32[]{:S(2)}) copy-start(f32[2,256]{1,0:T(2,128)} %param.23) | copy-start | bytes 6148
  25.4 36.2 %copy-start.26 = (f32[6,256]{1,0:T(8,128)S(1)}, f32[6,256]{1,0:T(8,128)}, u32[]{:S(2)}) copy-start(f32[6,256]{1,0:T(8,128)} %param.21) | copy-start | bytes 18436
  28.2 77.7 %copy-start.25 = (s32[1024]{0:T(1024)}, s32[1024]{0:T(1024)S(1)}, u32[]{:S(2)}) copy-start(s32[1024]{0:T(1024)S(1)} %pad_clamp_fusion.7) | copy-start | bytes 12292
  31.3 92.3 %copy-start.24 = (s32[1024]{0:T(1024)}, s32[1024]{0:T(1024)S(1)}, u32[]{:S(2)}) copy-start(s32[1024]{0:T(1024)S(1)} %pad_clamp_fusion.1) | copy-start | bytes 12292
  50.8 34.3 %all-to-all-start = ((bf16[128,4,320]{2,1,0:T(4,128)(2,1)}), bf16[128,4,320]{2,1,0:T(4,128)(2,1)S(1)}, u32[]{:S(2)}, u32[]{:S(2)}) async-start(bf16[128,4,320]{2,1,0:T(4,128)(2,1)} %reshape.191), calls=%async_computation | async-start | bytes 786432 | tf_op jit(solution)/shard_map/all_to_all | solution.py:117
  61.7 58.3 %copy-start.20 = (f32[1,256]{1,0:T(1,128)}, f32[1,256]{1,0:T(1,128)S(1)}, u32[]{:S(2)}) copy-start(f32[1,256]{1,0:T(1,128)S(1)} %get-tuple-element.12) | copy-start | bytes 3076
  61.7 58.3 %copy-start.22 = (f32[1,256]{1,0:T(1,128)}, f32[1,256]{1,0:T(1,128)S(1)}, u32[]{:S(2)}) copy-start(f32[1,256]{1,0:T(1,128)S(1)} %get-tuple-element.11) | copy-start | bytes 3076
  63.2 38.6 %copy-start.4 = (bf16[256,320]{0,1:T(8,128)(2,1)}, bf16[256,320]{0,1:T(8,128)(2,1)S(1)}, u32[]{:S(2)}) copy-start(bf16[256,320]{0,1:T(8,128)(2,1)S(1)} %copy.114) | copy-start | bytes 491524
  86.6 15.2 %copy-start.7 = (bf16[256,320]{0,1:T(8,128)(2,1)}, bf16[256,320]{0,1:T(8,128)(2,1)S(1)}, u32[]{:S(2)}) copy-start(bf16[256,320]{0,1:T(8,128)(2,1)S(1)} %copy.112) | copy-start | bytes 491524
  86.7 16.5 %collective-permute-start = (bf16[256,320]{0,1:T(8,128)(2,1)S(1)}, bf16[256,320]{0,1:T(8,128)(2,1)S(1)}, u32[]{:S(2)}, u32[]{:S(2)}) collective-permute-start(bf16[256,320]{0,1:T(8,128)(2,1)S(1)} %get-tuple-element.8), channel_id=1, source_target_pairs={{508,0},{0,4},{4,8},{8,12},{12,16},{16,20},{20,24},{24,28},{28,32}... | collective-permute-start | bytes 491528 | tf_op jit(solution)/shard_map/ppermute | solution.py:10
  88.6 14.6 %collective-permute-start.1 = (bf16[256,320]{0,1:T(8,128)(2,1)S(1)}, bf16[256,320]{0,1:T(8,128)(2,1)S(1)}, u32[]{:S(2)}, u32[]{:S(2)}) collective-permute-start(bf16[256,320]{0,1:T(8,128)(2,1)S(1)} %get-tuple-element.8), channel_id=1, source_target_pairs={{4,0},{8,4},{12,8},{16,12},{20,16},{24,20},{28,24},{32,28},{36,32}... | collective-permute-start | bytes 491528 | tf_op jit(solution)/shard_map/ppermute | solution.py:10
  96.8 5.1 %copy-start.13 = (bf16[320,320]{1,0:T(8,128)(2,1)S(1)}, bf16[320,320]{1,0:T(8,128)(2,1)}, u32[]{:S(2)}) copy-start(bf16[320,320]{1,0:T(8,128)(2,1)} %param.18) | copy-start | bytes 614404
  96.8 26.3 %all-to-all-start.2 = ((f32[4,256,320]{1,2,0:T(8,128)}), f32[4,256,320]{1,2,0:T(8,128)S(1)}, u32[]{:S(2)}, u32[]{:S(2)}) async-start(f32[4,256,320]{1,2,0:T(8,128)} %stack.4), calls=%async_computation.2 | async-start | bytes 2621440 | tf_op jit(solution)/shard_map/all_to_all | solution.py:134
  105.9 1.0 copy-start.29
  107.9 1.3 copy-start.31
  110.3 1.3 copy-start.35
  112.7 1.3 copy-start.37
  115.0 1.3 copy-start.39
  117.3 1.3 copy-start.33
  124.7 1.5 copy-start.5
  124.7 1.5 copy-start.8
  124.8 1.5 copy-start.11
  124.8 1.5 copy-start.14
  124.8 1.5 copy-start.42
  124.8 1.5 copy-start.44
  124.8 1.5 copy-start.46
  124.8 1.5 copy-start.48
  127.9 14.9 %copy-start.16 = (bf16[256,320]{0,1:T(8,128)(2,1)}, bf16[256,320]{0,1:T(8,128)(2,1)S(1)}, u32[]{:S(2)}) copy-start(bf16[256,320]{0,1:T(8,128)(2,1)S(1)} %get-tuple-element.27) | copy-start | bytes 491524
  127.9 16.2 %collective-permute-start.2 = (bf16[256,320]{0,1:T(8,128)(2,1)S(1)}, bf16[256,320]{0,1:T(8,128)(2,1)S(1)}, u32[]{:S(2)}, u32[]{:S(2)}) collective-permute-start(bf16[256,320]{0,1:T(8,128)(2,1)S(1)} %get-tuple-element.27), channel_id=1, source_target_pairs={{508,0},{0,4},{4,8},{8,12},{12,16},{16,20},{20,24},{24,28},{28,32}... | collective-permute-start | bytes 491528 | tf_op jit(solution)/shard_map/ppermute | solution.py:10
  129.9 14.3 %collective-permute-start.3 = (bf16[256,320]{0,1:T(8,128)(2,1)S(1)}, bf16[256,320]{0,1:T(8,128)(2,1)S(1)}, u32[]{:S(2)}, u32[]{:S(2)}) collective-permute-start(bf16[256,320]{0,1:T(8,128)(2,1)S(1)} %get-tuple-element.27), channel_id=1, source_target_pairs={{4,0},{8,4},{12,8},{16,12},{20,16},{24,20},{28,24},{32,28},{36,32}... | collective-permute-start | bytes 491528 | tf_op jit(solution)/shard_map/ppermute | solution.py:10
  138.0 25.9 %all-to-all-start.3 = ((f32[4,256,320]{1,2,0:T(8,128)}), f32[4,256,320]{1,2,0:T(8,128)S(1)}, u32[]{:S(2)}, u32[]{:S(2)}) async-start(f32[4,256,320]{1,2,0:T(8,128)} %stack.5), calls=%async_computation.3 | async-start | bytes 2621440 | tf_op jit(solution)/shard_map/all_to_all | solution.py:134
  155.4 1.1 copy-start.40
  156.5 2.1 %copy-start.3 = (f32[256,320]{1,0:T(8,128)S(1)}, f32[256,320]{1,0:T(8,128)}, u32[]{:S(2)}) copy-start(f32[256,320]{1,0:T(8,128)} %gather_fusion.13) | copy-start | bytes 983044
  156.6 2.1 %copy-start.38 = (pred[256]{0:T(512)(128)(4,1)S(1)}, pred[256]{0:T(512)(128)(4,1)}, u32[]{:S(2)}) copy-start(pred[256]{0:T(512)(128)(4,1)} %compare_and_fusion.4) | copy-start | bytes 772
  158.7 0.7 copy-start.23
  158.7 1.3 copy-start.2
  158.7 1.3 copy-start.36
  159.4 1.0 copy-start.21
  160.0 1.0 copy-start.1
  160.0 1.0 copy-start.32
  160.4 1.0 copy-start.30
  161.4 0.6 copy-start.34
  162.1 1.5 copy-start.10
  166.6 0.9 copy-start.6
  166.6 1.0 copy-start.9
  166.6 1.1 copy-start.12
  166.6 1.2 copy-start.15
  166.7 1.2 copy-start.17
  166.7 1.2 copy-start.43
  166.7 1.2 copy-start.45
  166.7 1.2 copy-start.47
  166.7 1.2 copy-start.49
